TPU v7x, 256 devices: a whole 4x4x8 slice. The times are simulated.
256 devices in a mesh: grp: 2 (over core), seq: 16 (over y, x), tp: 8 (over z).
Axes of the slice: x: 4, y: 4, z: 8, core: 2. Of those that a mesh axis runs over, the one named last changes fastest.
Arguments:
- prompt: bfloat16 [16384, 8192], P(('grp', 'seq'), 'tp'), may hold values from -6 to 6
- w_kv: bfloat16 [8192, 2048], P(None, 'tp'), may hold values from -0.0625 to 0.0625
- block_owner: int32 [2048, 1], P(('grp', 'seq')), may hold values from 0 to 31, as said below
- block_row: int32 [2048], P(('grp', 'seq')), may hold values from 0 to 31, as said below
- queries: bfloat16 [1024, 4, 8192], P(('grp', 'seq'), None, 'tp'), may hold values from -150 to 150
- new_kv: bfloat16 [1024, 4, 2048], P(('grp', 'seq'), None, 'tp'), may hold values from -6 to 6
- cache_codes: bfloat16 [1024, 128, 2048], P(('grp', 'seq'), None, 'tp'), may hold values from -4 to 4
- cache_scales: float32 [1024, 8, 16], P(('grp', 'seq'), None, 'tp'), may hold values from 0.5 to 2
- lengths: int32 [1024], P(('grp', 'seq')), may hold values from 1 to 128, 65536 in all
- w_out: bfloat16 [8192, 8192], P('tp', 'seq'), may hold values from -0.5 to 0.5
Outputs:
- mixed: bfloat16 [4096, 8192], P(('grp', 'tp'), 'seq')
Inputs may be any that keep to these rules, and one draw needn't show every extreme that they name: `block_owner`: the blocks come in aligned groups of 8 consecutive blocks that share one owner and one request; the groups of one prefill device all go to different owners, so a prefill device sends exactly 8 blocks to each owner it sends to. `block_row`: equal on all blocks of one aligned group of 8 blocks.
All inputs are finite; a program needn't handle non-finite values. No bound on the sum of `lengths` on one device may be relied on, other than what follows from the above.
Results may differ from a plain program's by a relative error of at most 0.014.
Values may be sent and summed in bfloat16 or wider, within the bound.
No kernel may reach another device: no remote copies, remote signals or barrier semaphores. Data moves between devices by JAX's collectives and lax.ppermute only.
A program may use at most 256 MiB of HBM per device.

v0:
```python
import math
import jax
import jax.numpy as jnp
from jax import lax
from jax.sharding import PartitionSpec as P

HQ = 64
KVH = 8
HD = 128
NEW = 4
BLK = 8
CBLK = 16
CAP = 8
EPS = 1e-05


def on_device(
    prompt, w_kv, block_owner, block_row, queries, new_kv, cache_codes, cache_scales, lengths, w_out
):
    group_count = lax.axis_size("grp")
    seq_count = lax.axis_size("seq")
    owners = group_count * seq_count
    tokens = prompt.shape[0]
    features = w_kv.shape[0]
    columns = w_kv.shape[1]
    row_count = queries.shape[0]
    shard_piece = lax.all_gather(prompt, "tp", axis=1, tiled=True)
    running = jnp.dot(shard_piece, w_kv, preferred_element_type=jnp.float32)
    widened = shard_piece.astype(jnp.float32)
    squares = jnp.sum(widened * widened, axis=1)
    row_scale = lax.rsqrt(squares / features + EPS)
    prompt_kv = (running * row_scale[:, None]).astype(jnp.bfloat16)
    blocks = tokens // BLK
    capacity = CAP
    owner_ids = block_owner[:, 0]
    owner_onehot = (owner_ids[:, None] == jnp.arange(owners, dtype=jnp.int32)[None, :]).astype(
        jnp.int32
    )
    slot_rank = jnp.sum((jnp.cumsum(owner_onehot, axis=0) - owner_onehot) * owner_onehot, axis=1)
    target = owner_ids * capacity + slot_rank
    chosen = target[None, :] == jnp.arange(owners * capacity, dtype=jnp.int32)[:, None]
    packed = jnp.dot(
        chosen.astype(jnp.bfloat16),
        prompt_kv.reshape(blocks, BLK * columns),
        preferred_element_type=jnp.float32,
    )
    send_kv = packed.astype(jnp.bfloat16).reshape(owners, capacity, BLK, columns)
    send_rows = (jnp.sum(jnp.where(chosen, block_row[None, :] + 1, 0), axis=1) - 1).reshape(
        owners, capacity
    )
    arrived_kv, arrived_rows = (
        lax.all_to_all(send_kv, ("grp", "seq"), split_axis=0, concat_axis=0, tiled=True),
        lax.all_to_all(send_rows, ("grp", "seq"), split_axis=0, concat_axis=0, tiled=True),
    )
    slots = arrived_rows.shape[1]
    kv_heads = columns // (2 * HD)
    head_group = HQ // KVH
    context = cache_codes.shape[1]
    query_heads = queries.reshape(row_count, NEW, kv_heads, head_group, HD)
    fresh_kv = new_kv.reshape(row_count, NEW, kv_heads, 2, HD)
    stored = cache_codes.reshape(row_count, context, kv_heads, 2, HD)
    block_scales = cache_scales.reshape(row_count, context // CBLK, kv_heads, 2)
    key_scale = jnp.transpose(jnp.repeat(block_scales[:, :, :, 0], CBLK, axis=1), (0, 2, 1))
    value_scale = jnp.transpose(jnp.repeat(block_scales[:, :, :, 1], CBLK, axis=1), (0, 2, 1))
    arrived = arrived_kv.reshape(owners * slots * BLK, kv_heads, 2, HD)
    arrived_targets = jnp.broadcast_to(arrived_rows[:, :, None], (owners, slots, BLK)).reshape(
        owners * slots * BLK
    )
    inverse_root = 1.0 / math.sqrt(HD)
    row_ids = jnp.arange(row_count, dtype=jnp.int32)
    s_cache = jnp.einsum(
        "rinhd,rpnd->rinhp", query_heads, stored[:, :, :, 0, :], preferred_element_type=jnp.float32
    )
    s_cache = s_cache * key_scale[:, None, :, None, :] * inverse_root
    cache_live = jnp.arange(context, dtype=jnp.int32)[None, :] < lengths[:, None]
    s_cache = jnp.where(cache_live[:, None, None, None, :], s_cache, -jnp.inf)
    s_sent = (
        jnp.einsum(
            "rinhd,knd->rinhk", query_heads, arrived[:, :, 0, :], preferred_element_type=jnp.float32
        )
        * inverse_root
    )
    sent_live = arrived_targets[None, :] == row_ids[:, None]
    s_sent = jnp.where(sent_live[:, None, None, None, :], s_sent, -jnp.inf)
    s_fresh = (
        jnp.einsum(
            "rinhd,rjnd->rinhj",
            query_heads,
            fresh_kv[:, :, :, 0, :],
            preferred_element_type=jnp.float32,
        )
        * inverse_root
    )
    causal = jnp.arange(NEW)[None, :] <= jnp.arange(NEW)[:, None]
    s_fresh = jnp.where(causal[None, :, None, None, :], s_fresh, -jnp.inf)
    row_max = jnp.maximum(
        jnp.maximum(jnp.max(s_cache, axis=-1), jnp.max(s_sent, axis=-1)), jnp.max(s_fresh, axis=-1)
    )
    w_cache = jnp.exp(s_cache - row_max[..., None])
    w_sent = jnp.exp(s_sent - row_max[..., None])
    w_fresh = jnp.exp(s_fresh - row_max[..., None])
    denominator = jnp.sum(w_cache, axis=-1) + jnp.sum(w_sent, axis=-1) + jnp.sum(w_fresh, axis=-1)
    cache_weights = (w_cache * value_scale[:, None, :, None, :]).astype(jnp.bfloat16)
    numerator = jnp.einsum(
        "rinhp,rpnd->rinhd",
        cache_weights,
        stored[:, :, :, 1, :],
        preferred_element_type=jnp.float32,
    )
    numerator = numerator + jnp.einsum(
        "rinhk,knd->rinhd",
        w_sent.astype(jnp.bfloat16),
        arrived[:, :, 1, :],
        preferred_element_type=jnp.float32,
    )
    numerator = numerator + jnp.einsum(
        "rinhj,rjnd->rinhd",
        w_fresh.astype(jnp.bfloat16),
        fresh_kv[:, :, :, 1, :],
        preferred_element_type=jnp.float32,
    )
    attention = (
        (numerator / denominator[..., None])
        .astype(jnp.bfloat16)
        .reshape(row_count * NEW, kv_heads * head_group * HD)
    )
    head_terms = jnp.dot(
        lax.all_gather(attention, "seq", axis=0, tiled=True),
        w_out,
        preferred_element_type=jnp.float32,
    )
    return lax.psum_scatter(head_terms.astype(jnp.bfloat16), "tp", scatter_dimension=0, tiled=True)


def solution(mesh):
    in_specs = (
        P(("grp", "seq"), "tp"),
        P(None, "tp"),
        P(("grp", "seq"), None),
        P(("grp", "seq")),
        P(("grp", "seq"), None, "tp"),
        P(("grp", "seq"), None, "tp"),
        P(("grp", "seq"), None, "tp"),
        P(("grp", "seq"), None, "tp"),
        P(("grp", "seq")),
        P("tp", "seq"),
    )
    out_specs = P(("grp", "tp"), "seq")
    return jax.shard_map(
        on_device, mesh=mesh, in_specs=in_specs, out_specs=out_specs, check_vma=False
    )
```

profile of v0, /device:TPU:2, one launch (start us, length us, event | category | flops | bytes accessed | tf_op | source)
XLA Modules:
  0.0 270.8 jit_solution(4735549890900812305)
XLA Ops:
  6.6 0.7 all-gather.3.cloned.1.call-update
  7.3 0.7 fusion.33
  8.1 0.8 select_reduce_fusion.1
  10.4 0.7 sub.35
  11.1 7.6 %all-to-all-start = ((s32[32,1,8]{2,1,0:T(1,128)}), s32[32,1,8]{2,1,0:T(1,128)S(1)}, u32[]{:S(2)}, u32[]{:S(2)}) async-start(s32[32,1,8]{2,1,0:T(1,128)} %bitcast.10), calls=%async_computation | async-start | bytes 32768 | tf_op jit(solution)/shard_map/all_to_all | solution.py:53
  18.7 1.1 reshape.223
  19.8 4.1 %copy.64 = bf16[32,128,256]{1,2,0:T(8,128)(2,1)} copy(bf16[32,128,256]{2,1,0:T(8,128)(2,1)} %param.16) | data formatting | bytes 4194304 | tf_op args[6]
  24.2 82.0 %all-gather.3.cloned.1.call-done = bf16[512,8192]{1,0:T(8,128)(2,1)} async-done(((bf16[512,1024]{1,0:T(8,128)(2,1)}), bf16[512,8192]{1,0:T(8,128)(2,1)}) %all-gather.3.cloned.1.call-update) | async-done | bytes 8388624 | tf_op jit(solution)/shard_map/all_gather | solution.py:27
  106.2 5.3 %multiply_reduce_fusion = f32[512]{0:T(512)S(1)} fusion(bf16[512,8192]{1,0:T(8,128)(2,1)} %all-gather.3.cloned.1.call-done), kind=kLoop, calls=%fused_computation | loop fusion | flops 12582400 | bytes 8390656 | tf_op jit(solution)/shard_map/reduce_sum | solution.py:30
  112.0 4.6 %fusion.16 = bf16[512,256]{1,0:T(8,128)(2,1)S(1)} fusion(bf16[512,8192]{1,0:T(8,128)(2,1)S(1)} %copy-done.1, bf16[8192,256]{1,0:T(8,128)(2,1)} %param.11, f32[512]{0:T(512)S(1)} %add_rsqrt_fusion), kind=kOutput, calls=%fused_computation.23 | convolution fusion | flops 2147745792 | bytes 12847104 | tf_op jit(solution)/shard_map/dot_general | solution.py:28
  117.2 1.3 copy.68
  118.5 7.4 %all-to-all-start.1 = ((bf16[32,8,8,256]{3,2,1,0:T(8,128)(2,1)}), bf16[32,8,8,256]{3,2,1,0:T(8,128)(2,1)S(1)}, u32[]{:S(2)}, u32[]{:S(2)}) async-start(bf16[32,8,8,256]{3,2,1,0:T(8,128)(2,1)} %copy.68), calls=%async_computation.1 | async-start | bytes 2097152 | tf_op jit(solution)/shard_map/all_to_all | solution.py:52
  126.2 2.6 fusion.37
  128.8 3.0 %fusion.38 = (f32[32,4,8]{2,1,0:T(4,128)}, f32[32,4,1,8,128]{4,3,1,0,2:T(8,128)}) fusion(f32[32,128]{1,0:T(8,128)S(1)} %copy.66, bf16[32,4,8,128]{3,2,1,0:T(8,128)(2,1)S(1)} %reshape.223, bf16[32,128,1,2,128]{1,4,3,0,2:T(8,128)(2,1)} %bitcast.147, pred[32,128]{1,0:T(8,128)(4,1)S(1)} %iota_compare_fusion.4), kind=kOutput, calls=%fused_computation.67 | convolution fusion | flops 34077696 | bytes 1859584 | tf_op jit(solution)/shard_map/rinhd,rpnd->rinhp/dot_general | solution.py:71
  132.1 9.2 %all-to-all-done.1 = bf16[32,8,8,256]{3,2,1,0:T(8,128)(2,1)S(1)} async-done(((bf16[32,8,8,256]{3,2,1,0:T(8,128)(2,1)}), bf16[32,8,8,256]{3,2,1,0:T(8,128)(2,1)S(1)}, u32[]{:S(2)}, u32[]{:S(2)}) %all-to-all-start.1) | async-done | bytes 1048608 | tf_op jit(solution)/shard_map/all_to_all | solution.py:52
  141.5 2.3 fusion.34
  143.9 4.6 %fusion.2 = (f32[32,4,8]{0,2,1:T(8,128)S(1)}, f32[2048,32,4,8]{0,1,3,2:T(8,128)}) fusion(pred[32,2048]{1,0:T(8,128)(4,1)S(1)} %iota_compare_fusion, bf16[32,4,8,128]{3,2,1,0:T(8,128)(2,1)S(1)} %reshape.223, bf16[2048,1,1,128]{3,2,0,1:T(2,128)(2,1)S(1)} %get-tuple-element.8), kind=kOutput, calls=%fused_computation.5 | convolution fusion | flops 543161344 | bytes 9244672 | tf_op jit(solution)/shard_map/rinhd,knd->rinhk/dot_general | solution.py:78
  148.6 5.9 %fusion = (f32[32,4,8]{0,2,1:T(8,128)S(1)}, bf16[32,4,8,2048]{3,0,2,1:T(8,128)(2,1)}) fusion(f32[2048,32,4,8]{0,1,3,2:T(8,128)} %get-tuple-element.18, f32[32,4,8]{0,2,1:T(8,128)S(1)} %copy.77, pred[32,2048]{1,0:T(8,128)(4,1)S(1)} %iota_compare_fusion), kind=kLoop, calls=%fused_computation.3 | loop fusion | flops 10484736 | bytes 12656640 | tf_op jit(solution)/shard_map/reduce_sum | solution.py:102
  155.6 5.1 %fusion.13 = f32[32,4,1,8,128]{4,3,1,0,2:T(8,128)S(1)} fusion(bf16[32,4,8,2048]{3,0,2,1:T(8,128)(2,1)} %get-tuple-element.6, bf16[2048,1,1,128]{3,2,0,1:T(2,128)(2,1)S(1)} %copy-done.4), kind=kOutput, calls=%fused_computation.21 | convolution fusion | flops 536870912 | bytes 5242880 | tf_op jit(solution)/shard_map/rinhk,knd->rinhd/dot_general | solution.py:110
  160.8 0.7 fusion.17
  161.5 0.8 copy.120
  162.3 53.3 %all-gather.5.cloned.1.call-done = bf16[2048,1024]{1,0:T(8,128)(2,1)} async-done(((bf16[128,1024]{1,0:T(8,128)(2,1)}), bf16[2048,1024]{1,0:T(8,128)(2,1)}) %all-gather.5.cloned.1.call-update) | async-done | bytes 4194320 | tf_op jit(solution)/shard_map/all_gather | solution.py:128
  215.7 5.9 %convolution_convert_fusion = bf16[2048,512]{1,0:T(8,128)(2,1)} fusion(bf16[2048,1024]{1,0:T(8,128)(2,1)} %all-gather.5.cloned.1.call-done, bf16[1024,512]{1,0:T(8,128)(2,1)S(1)} %copy-done), kind=kOutput, calls=%fused_computation.9 | convolution fusion | flops 2148532224 | bytes 7340032 | tf_op jit(solution)/shard_map/dot_general | solution.py:127
  221.5 42.8 %reduce-scatter.2.cloned.1.call-done = bf16[256,512]{1,0:T(8,128)(2,1)} async-done(((bf16[2048,512]{1,0:T(8,128)(2,1)}), bf16[256,512]{1,0:T(8,128)(2,1)}) %reduce-scatter.2.cloned.1.call-update) | async-done | bytes 262160 | tf_op jit(solution)/shard_map/reduce_scatter | solution.py:132
  (57 shorter events, 5.2 us)
Async XLA Ops:
  6.5 209.1 %copy-start = (bf16[1024,512]{1,0:T(8,128)(2,1)S(1)}, bf16[1024,512]{1,0:T(8,128)(2,1)}, u32[]{:S(2)}) copy-start(bf16[1024,512]{1,0:T(8,128)(2,1)} %param.19) | copy-start | bytes 3145732
  6.5 17.3 %copy-start.9 = (f32[32,8,2]{0,2,1:T(2,128)S(1)}, f32[32,8,2]{0,2,1:T(2,128)}, u32[]{:S(2)}) copy-start(f32[32,8,2]{0,2,1:T(2,128)} %param.17) | copy-start | bytes 6148
  6.5 17.4 %copy-start.6 = (bf16[32,4,256]{2,1,0:T(4,128)(2,1)S(1)}, bf16[32,4,256]{2,1,0:T(4,128)(2,1)}, u32[]{:S(2)}) copy-start(bf16[32,4,256]{2,1,0:T(4,128)(2,1)} %param.15) | copy-start | bytes 196612
  6.5 17.5 %copy-start.10 = (s32[32]{0:T(128)S(1)}, s32[32]{0:T(128)}, u32[]{:S(2)}) copy-start(s32[32]{0:T(128)} %param.18) | copy-start | bytes 388
  6.5 99.7 %all-gather.3.cloned.1.call-start = ((), (), s32[]{:S(2)}) async-start(), calls=%async_computation.3 | async-start | bytes 9437184 | tf_op jit(solution)/shard_map/all_gather | solution.py:27
  11.1 107.4 %all-to-all-start = ((s32[32,1,8]{2,1,0:T(1,128)}), s32[32,1,8]{2,1,0:T(1,128)S(1)}, u32[]{:S(2)}, u32[]{:S(2)}) async-start(s32[32,1,8]{2,1,0:T(1,128)} %bitcast.10), calls=%async_computation | async-start | bytes 32768 | tf_op jit(solution)/shard_map/all_to_all | solution.py:53
  106.2 5.8 %copy-start.1 = (bf16[512,8192]{1,0:T(8,128)(2,1)S(1)}, bf16[512,8192]{1,0:T(8,128)(2,1)}, u32[]{:S(2)}) copy-start(bf16[512,8192]{1,0:T(8,128)(2,1)} %all-gather.3.cloned.1.call-done) | copy-start | bytes 25165828
  118.5 22.8 %all-to-all-start.1 = ((bf16[32,8,8,256]{3,2,1,0:T(8,128)(2,1)}), bf16[32,8,8,256]{3,2,1,0:T(8,128)(2,1)S(1)}, u32[]{:S(2)}, u32[]{:S(2)}) async-start(bf16[32,8,8,256]{3,2,1,0:T(8,128)(2,1)} %copy.68), calls=%async_computation.1 | async-start | bytes 2097152 | tf_op jit(solution)/shard_map/all_to_all | solution.py:52
  125.9 89.7 %all-gather.5.cloned.1.call-start = ((), (), s32[]{:S(2)}) async-start(), calls=%async_computation.4 | async-start | bytes 4456448 | tf_op jit(solution)/shard_map/all_gather | solution.py:128
  143.8 4.7 %copy-start.7 = (f32[32,4,8]{2,1,0:T(4,128)S(1)}, f32[32,4,8]{2,1,0:T(4,128)}, u32[]{:S(2)}) copy-start(f32[32,4,8]{2,1,0:T(4,128)} %get-tuple-element.13) | copy-start | bytes 12292
  143.9 4.7 %copy-start.8 = (f32[32,4,8]{2,1,0:T(4,128)S(1)}, f32[32,4,8]{2,1,0:T(4,128)}, u32[]{:S(2)}) copy-start(f32[32,4,8]{2,1,0:T(4,128)} %get-tuple-element.15) | copy-start | bytes 12292
  148.6 6.0 %copy-start.5 = (f32[32,4,1,8,128]{4,3,1,0,2:T(8,128)S(1)}, f32[32,4,1,8,128]{4,3,1,0,2:T(8,128)}, u32[]{:S(2)}) copy-start(f32[32,4,1,8,128]{4,3,1,0,2:T(8,128)} %get-tuple-element.16) | copy-start | bytes 1572868
  148.6 6.4 %copy-start.3 = (f32[32,4,1,8,4]{3,4,1,0,2:T(4,128)S(1)}, f32[32,4,1,8,4]{3,4,1,0,2:T(4,128)}, u32[]{:S(2)}) copy-start(f32[32,4,1,8,4]{3,4,1,0,2:T(4,128)} %get-tuple-element.14) | copy-start | bytes 49156
  148.6 7.0 %copy-start.4 = (bf16[2048,1,1,128]{3,2,0,1:T(2,128)(2,1)S(1)}, bf16[2048,1,1,128]{3,2,0,1:T(2,128)(2,1)}, u32[]{:S(2)}) copy-start(bf16[2048,1,1,128]{3,2,0,1:T(2,128)(2,1)} %get-tuple-element.7) | copy-start | bytes 1572868
  155.6 5.1 %copy-start.2 = (bf16[32,128,256]{1,2,0:T(8,128)(2,1)S(1)}, bf16[32,128,256]{1,2,0:T(8,128)(2,1)}, u32[]{:S(2)}) copy-start(bf16[32,128,256]{1,2,0:T(8,128)(2,1)} %copy.64) | copy-start | bytes 6291460
  162.3 102.0 %reduce-scatter.2.cloned.1.call-start = ((), (), s32[]{:S(2)}) async-start(), calls=%async_computation.5 | async-start | bytes 2359296 | tf_op jit(solution)/shard_map/reduce_scatter | solution.py:132
Sparse Core Ops, SparseCore 0:
  9.1 97.0 all-gather.2
  162.4 53.2 all-gather.4
  221.7 42.5 reduce-scatter.1
where the time goes:
time: 271 us
  waiting for transfers between devices  188 us (69%)
  matrix products  27.3 us (10%)
  starting transfers between devices  15.3 us (6%)
  other arithmetic  15.1 us (6%)
  between operations  13.3 us (5%)
  local copies, waits for them, and re-layouts  11.8 us (4%)
    all_gather x1, waiting for transfers between devices, on_device(): shard_piece = lax.all_gather(prompt, 'tp', axis=1, tiled=True)  82 us
    all_gather x1, waiting for transfers between devices, on_device(): lax.all_gather(attention, 'seq', axis=0, tiled=True)  53.3 us
    reduce_scatter x1, waiting for transfers between devices, on_device(): lax.psum_scatter(head_terms.astype(jnp.bfloat16), 'tp', scatter_dimension...  42.8 us
    all_to_all x1, waiting for transfers between devices, on_device(): lax.all_to_all(send_kv, ('grp', 'seq'), split_axis=0, concat_axis=0, tile...  9.17 us
    all_to_all x1, starting transfers between devices, on_device(): lax.all_to_all(send_rows, ('grp', 'seq'), split_axis=0, concat_axis=0, ti...  7.62 us
    all_to_all x1, starting transfers between devices, on_device(): lax.all_to_all(send_kv, ('grp', 'seq'), split_axis=0, concat_axis=0, tile...  7.41 us
    reduce_sum x1, other arithmetic, on_device(): jnp.sum(w_sent, axis=-1)  5.9 us
    dot_general x1, matrix products, on_device(): jnp.dot(lax.all_gather(attention, 'seq', axis=0, tiled=True), w_out, pref...  5.86 us
  transfers between devices with their start and end apart: 5, of which 4 were waited for; matrix products, arithmetic and copies ran while one was open for 10% of the time, Pallas kernels for 0%

commit v1 on v0

--- a/solution.py
+++ b/solution.py
@@ -24,7 +24,9 @@
     features = w_kv.shape[0]
     columns = w_kv.shape[1]
     row_count = queries.shape[0]
-    shard_piece = lax.all_gather(prompt, "tp", axis=1, tiled=True)
+    shard_piece = jnp.concatenate(
+        lax.all_to_all(jnp.stack([prompt] * lax.axis_size("tp")), "tp", 0, 0), axis=1
+    )
     running = jnp.dot(shard_piece, w_kv, preferred_element_type=jnp.float32)
     widened = shard_piece.astype(jnp.float32)
     squares = jnp.sum(widened * widened, axis=1)

time: 271 us -> 379 us (1.40)
  waiting for transfers between devices: 188 us -> 283 us
  starting transfers between devices: 15.3 us -> 23.8 us
  local copies, waits for them, and re-layouts: 11.8 us -> 16.1 us
    all_to_all x0 -> x1, waiting for transfers between devices: none -> 181 us  [on_device(): lax.all_to_all(jnp.stack([prompt] * lax.axis_size('tp')), 'tp', 0, 0)]
    all_gather x1 -> x0, waiting for transfers between devices: 82 us -> none  [on_device(): shard_piece = lax.all_gather(prompt, 'tp', axis=1, tiled=True)]
    all_to_all x0 -> x1, starting transfers between devices: none -> 8.6 us  [on_device(): lax.all_to_all(jnp.stack([prompt] * lax.axis_size('tp')), 'tp', 0, 0)]
    another operation x1 -> x2, local copies, waits for them, and re-layouts: 1.05 us -> 4.99 us  [the longest x1 3.94 us: on_device(): jnp.stack([prompt] * lax.axis_size('tp'))]
  transfers between devices with their start and end apart: 5 -> 5, of which waited for: 4 -> 4; matrix products, arithmetic and copies ran while one was open for 10% -> 6% of each run, Pallas kernels for 0% -> 0%
where the time goes in v1:
time: 379 us; the launch traced here: 378 us
  waiting for transfers between devices  283 us (75%)
  matrix products  28.5 us (8%)
  starting transfers between devices  23.8 us (6%)
  local copies, waits for them, and re-layouts  16.1 us (4%)
  between operations  13.7 us (4%)
  other arithmetic  12.6 us (3%)
    all_to_all x1, waiting for transfers between devices, on_device(): lax.all_to_all(jnp.stack([prompt] * lax.axis_size('tp')), 'tp', 0, 0)  181 us
    all_gather x1, waiting for transfers between devices, on_device(): lax.all_gather(attention, 'seq', axis=0, tiled=True)  50.8 us
    reduce_scatter x1, waiting for transfers between devices, on_device(): lax.psum_scatter(head_terms.astype(jnp.bfloat16), 'tp', scatter_dimension...  42.6 us
    all_to_all x1, waiting for transfers between devices, on_device(): lax.all_to_all(send_kv, ('grp', 'seq'), split_axis=0, concat_axis=0, tile...  9.2 us
    all_to_all x1, starting transfers between devices, on_device(): lax.all_to_all(jnp.stack([prompt] * lax.axis_size('tp')), 'tp', 0, 0)  8.6 us
    all_to_all x1, starting transfers between devices, on_device(): lax.all_to_all(send_rows, ('grp', 'seq'), split_axis=0, concat_axis=0, ti...  7.62 us
  transfers between devices with their start and end apart: 5, of which 4 were waited for; matrix products, arithmetic and copies ran while one was open for 6% of the time, Pallas kernels for 0%

profile of v1, /device:TPU:2, one launch (start us, length us, event | category | flops | bytes accessed | tf_op | source)
XLA Modules:
  0.0 378.0 jit_solution(4311334833487350173)
XLA Ops:
  6.5 1.6 copy.71
  8.1 3.9 %stack.2 = bf16[8,512,1024]{1,2,0:T(8,128)(2,1)} broadcast(bf16[512,1024]{0,1:T(8,128)(2,1)S(1)} %copy.71), dimensions={1,2} | broadcast | bytes 9437184 | tf_op jit(solution)/shard_map/stack | solution.py:28
  12.1 8.6 %all-to-all-start.1 = ((bf16[8,512,1024]{1,2,0:T(8,128)(2,1)}), bf16[8,512,1024]{1,2,0:T(8,128)(2,1)}, u32[]{:S(2)}, u32[]{:S(2)}) async-start(bf16[8,512,1024]{1,2,0:T(8,128)(2,1)} %stack.2), calls=%async_computation.1 | async-start | bytes 16777216 | tf_op jit(solution)/shard_map/all_to_all | solution.py:28
  21.6 0.7 sub.35
  22.3 1.1 reshape.231
  23.4 2.9 copy.67
  26.7 180.6 %all-to-all-done.1 = bf16[8,512,1024]{1,2,0:T(8,128)(2,1)} async-done(((bf16[8,512,1024]{1,2,0:T(8,128)(2,1)}), bf16[8,512,1024]{1,2,0:T(8,128)(2,1)}, u32[]{:S(2)}, u32[]{:S(2)}) %all-to-all-start.1) | async-done | bytes 8388640 | tf_op jit(solution)/shard_map/all_to_all | solution.py:28
  207.3 7.6 %all-to-all-start = ((s32[32,1,8]{2,1,0:T(1,128)}), s32[32,1,8]{2,1,0:T(1,128)S(1)}, u32[]{:S(2)}, u32[]{:S(2)}) async-start(s32[32,1,8]{2,1,0:T(1,128)} %bitcast.10), calls=%async_computation | async-start | bytes 32768 | tf_op jit(solution)/shard_map/all_to_all | solution.py:55
  214.9 5.3 %multiply_reduce_fusion = f32[512]{0:T(512)S(1)} fusion(bf16[8,512,1024]{1,2,0:T(8,128)(2,1)} %all-to-all-done.1), kind=kLoop, calls=%fused_computation | loop fusion | flops 12582400 | bytes 8390656 | tf_op jit(solution)/shard_map/reduce_sum | solution.py:32
  220.3 5.8 %fusion.17 = bf16[512,256]{1,0:T(8,128)(2,1)S(1)} fusion(bf16[512,8192]{0,1:T(8,128)(2,1)} %bitcast.13, bf16[8192,256]{1,0:T(8,128)(2,1)S(1)} %copy-done.1, f32[512]{0:T(512)S(1)} %add_rsqrt_fusion), kind=kOutput, calls=%fused_computation.24 | convolution fusion | flops 2147745792 | bytes 12847104 | tf_op jit(solution)/shard_map/dot_general | solution.py:30
  226.7 1.3 copy.72
  228.0 7.4 %all-to-all-start.2 = ((bf16[32,8,8,256]{3,2,1,0:T(8,128)(2,1)}), bf16[32,8,8,256]{3,2,1,0:T(8,128)(2,1)S(1)}, u32[]{:S(2)}, u32[]{:S(2)}) async-start(bf16[32,8,8,256]{3,2,1,0:T(8,128)(2,1)} %copy.72), calls=%async_computation.2 | async-start | bytes 2097152 | tf_op jit(solution)/shard_map/all_to_all | solution.py:54
  235.6 2.6 fusion.37
  238.2 3.0 fusion.38
  241.5 9.2 %all-to-all-done.2 = bf16[32,8,8,256]{3,2,1,0:T(8,128)(2,1)S(1)} async-done(((bf16[32,8,8,256]{3,2,1,0:T(8,128)(2,1)}), bf16[32,8,8,256]{3,2,1,0:T(8,128)(2,1)S(1)}, u32[]{:S(2)}, u32[]{:S(2)}) %all-to-all-start.2) | async-done | bytes 1048608 | tf_op jit(solution)/shard_map/all_to_all | solution.py:54
  251.0 2.3 fusion.34
  253.3 4.6 %fusion.2 = (f32[32,4,8]{0,2,1:T(8,128)S(1)}, f32[2048,32,4,8]{0,1,3,2:T(8,128)}) fusion(pred[32,2048]{1,0:T(8,128)(4,1)S(1)} %iota_compare_fusion, bf16[32,4,8,128]{3,2,1,0:T(8,128)(2,1)S(1)} %reshape.231, bf16[2048,1,1,128]{3,2,0,1:T(2,128)(2,1)S(1)} %get-tuple-element.8), kind=kOutput, calls=%fused_computation.5 | convolution fusion | flops 543161344 | bytes 9244672 | tf_op jit(solution)/shard_map/rinhd,knd->rinhk/dot_general | solution.py:80
  258.1 5.9 %fusion = (f32[32,4,8]{0,2,1:T(8,128)S(1)}, bf16[32,4,8,2048]{3,0,2,1:T(8,128)(2,1)}) fusion(f32[2048,32,4,8]{0,1,3,2:T(8,128)} %get-tuple-element.18, f32[32,4,8]{0,2,1:T(8,128)S(1)} %copy.81, pred[32,2048]{1,0:T(8,128)(4,1)S(1)} %iota_compare_fusion), kind=kLoop, calls=%fused_computation.3 | loop fusion | flops 10484736 | bytes 12656640 | tf_op jit(solution)/shard_map/reduce_sum | solution.py:104
  265.1 5.1 %fusion.13 = f32[32,4,1,8,128]{4,3,1,0,2:T(8,128)S(1)} fusion(bf16[32,4,8,2048]{3,0,2,1:T(8,128)(2,1)} %get-tuple-element.6, bf16[2048,1,1,128]{3,2,0,1:T(2,128)(2,1)S(1)} %copy-done.5), kind=kOutput, calls=%fused_computation.21 | convolution fusion | flops 536870912 | bytes 5242880 | tf_op jit(solution)/shard_map/rinhk,knd->rinhd/dot_general | solution.py:112
  270.3 0.7 fusion.16
  271.0 0.8 copy.124
  271.8 50.8 %all-gather.2.cloned.1.call-done = bf16[2048,1024]{1,0:T(8,128)(2,1)} async-done(((bf16[128,1024]{1,0:T(8,128)(2,1)}), bf16[2048,1024]{1,0:T(8,128)(2,1)}) %all-gather.2.cloned.1.call-update) | async-done | bytes 4194320 | tf_op jit(solution)/shard_map/all_gather | solution.py:130
  322.7 5.8 %convolution_convert_fusion = bf16[2048,512]{1,0:T(8,128)(2,1)} fusion(bf16[2048,1024]{1,0:T(8,128)(2,1)} %all-gather.2.cloned.1.call-done, bf16[1024,512]{1,0:T(8,128)(2,1)S(1)} %copy-done), kind=kOutput, calls=%fused_computation.9 | convolution fusion | flops 2148532224 | bytes 7340032 | tf_op jit(solution)/shard_map/dot_general | solution.py:129
  328.5 42.6 %reduce-scatter.2.cloned.1.call-done = bf16[256,512]{1,0:T(8,128)(2,1)} async-done(((bf16[2048,512]{1,0:T(8,128)(2,1)}), bf16[256,512]{1,0:T(8,128)(2,1)}) %reduce-scatter.2.cloned.1.call-update) | async-done | bytes 262160 | tf_op jit(solution)/shard_map/reduce_scatter | solution.py:134
  (67 shorter events, 4.0 us)
Async XLA Ops:
  6.5 316.1 %copy-start = (bf16[1024,512]{1,0:T(8,128)(2,1)S(1)}, bf16[1024,512]{1,0:T(8,128)(2,1)}, u32[]{:S(2)}) copy-start(bf16[1024,512]{1,0:T(8,128)(2,1)} %param.19) | copy-start | bytes 3145732
  12.1 8.6 %copy-start.11 = (s32[64,1]{0,1:T(1,128)S(1)}, s32[64,1]{0,1:T(1,128)}, u32[]{:S(2)}) copy-start(s32[64,1]{0,1:T(1,128)} %param.12) | copy-start | bytes 772
  12.1 9.0 %copy-start.14 = (s32[64]{0:T(128)S(1)}, s32[64]{0:T(128)}, u32[]{:S(2)}) copy-start(s32[64]{0:T(128)} %param.13) | copy-start | bytes 772
  12.1 11.3 %copy-start.2 = (bf16[32,128,256]{2,1,0:T(8,128)(2,1)S(1)}, bf16[32,128,256]{2,1,0:T(8,128)(2,1)}, u32[]{:S(2)}) copy-start(bf16[32,128,256]{2,1,0:T(8,128)(2,1)} %param.16) | copy-start | bytes 6291460
  12.1 195.2 %all-to-all-start.1 = ((bf16[8,512,1024]{1,2,0:T(8,128)(2,1)}), bf16[8,512,1024]{1,2,0:T(8,128)(2,1)}, u32[]{:S(2)}, u32[]{:S(2)}) async-start(bf16[8,512,1024]{1,2,0:T(8,128)(2,1)} %stack.2), calls=%async_computation.1 | async-start | bytes 16777216 | tf_op jit(solution)/shard_map/all_to_all | solution.py:28
  20.7 5.6 %copy-start.10 = (f32[32,8,2]{0,2,1:T(2,128)S(1)}, f32[32,8,2]{0,2,1:T(2,128)}, u32[]{:S(2)}) copy-start(f32[32,8,2]{0,2,1:T(2,128)} %param.17) | copy-start | bytes 6148
  20.7 5.6 %copy-start.7 = (bf16[32,4,256]{2,1,0:T(4,128)(2,1)S(1)}, bf16[32,4,256]{2,1,0:T(4,128)(2,1)}, u32[]{:S(2)}) copy-start(bf16[32,4,256]{2,1,0:T(4,128)(2,1)} %param.15) | copy-start | bytes 196612
  20.7 5.8 %copy-start.15 = (s32[32]{0:T(128)S(1)}, s32[32]{0:T(128)}, u32[]{:S(2)}) copy-start(s32[32]{0:T(128)} %param.18) | copy-start | bytes 388
  21.1 0.5 copy-start.12
  207.3 20.7 %all-to-all-start = ((s32[32,1,8]{2,1,0:T(1,128)}), s32[32,1,8]{2,1,0:T(1,128)S(1)}, u32[]{:S(2)}, u32[]{:S(2)}) async-start(s32[32,1,8]{2,1,0:T(1,128)} %bitcast.10), calls=%async_computation | async-start | bytes 32768 | tf_op jit(solution)/shard_map/all_to_all | solution.py:55
  214.9 5.3 %copy-start.1 = (bf16[8192,256]{1,0:T(8,128)(2,1)S(1)}, bf16[8192,256]{1,0:T(8,128)(2,1)}, u32[]{:S(2)}) copy-start(bf16[8192,256]{1,0:T(8,128)(2,1)} %param.11) | copy-start | bytes 12582916
  220.3 5.9 %copy-start.13 = (s32[64]{0:T(128)S(1)}, s32[64]{0:T(128)}, u32[]{:S(2)}) copy-start(s32[64]{0:T(128)} %copy-done.12) | copy-start | bytes 772
  228.0 22.7 %all-to-all-start.2 = ((bf16[32,8,8,256]{3,2,1,0:T(8,128)(2,1)}), bf16[32,8,8,256]{3,2,1,0:T(8,128)(2,1)S(1)}, u32[]{:S(2)}, u32[]{:S(2)}) async-start(bf16[32,8,8,256]{3,2,1,0:T(8,128)(2,1)} %copy.72), calls=%async_computation.2 | async-start | bytes 2097152 | tf_op jit(solution)/shard_map/all_to_all | solution.py:54
  235.4 87.3 %all-gather.2.cloned.1.call-start = ((), (), s32[]{:S(2)}) async-start(), calls=%async_computation.4 | async-start | bytes 4456448 | tf_op jit(solution)/shard_map/all_gather | solution.py:130
  253.3 4.7 %copy-start.8 = (f32[32,4,8]{2,1,0:T(4,128)S(1)}, f32[32,4,8]{2,1,0:T(4,128)}, u32[]{:S(2)}) copy-start(f32[32,4,8]{2,1,0:T(4,128)} %get-tuple-element.13) | copy-start | bytes 12292
  253.3 4.7 %copy-start.9 = (f32[32,4,8]{2,1,0:T(4,128)S(1)}, f32[32,4,8]{2,1,0:T(4,128)}, u32[]{:S(2)}) copy-start(f32[32,4,8]{2,1,0:T(4,128)} %get-tuple-element.15) | copy-start | bytes 12292
  258.1 6.0 %copy-start.6 = (f32[32,4,1,8,128]{4,3,1,0,2:T(8,128)S(1)}, f32[32,4,1,8,128]{4,3,1,0,2:T(8,128)}, u32[]{:S(2)}) copy-start(f32[32,4,1,8,128]{4,3,1,0,2:T(8,128)} %get-tuple-element.16) | copy-start | bytes 1572868
  258.1 6.5 %copy-start.4 = (f32[32,4,1,8,4]{3,4,1,0,2:T(4,128)S(1)}, f32[32,4,1,8,4]{3,4,1,0,2:T(4,128)}, u32[]{:S(2)}) copy-start(f32[32,4,1,8,4]{3,4,1,0,2:T(4,128)} %get-tuple-element.14) | copy-start | bytes 49156
  258.1 7.0 %copy-start.5 = (bf16[2048,1,1,128]{3,2,0,1:T(2,128)(2,1)S(1)}, bf16[2048,1,1,128]{3,2,0,1:T(2,128)(2,1)}, u32[]{:S(2)}) copy-start(bf16[2048,1,1,128]{3,2,0,1:T(2,128)(2,1)} %get-tuple-element.7) | copy-start | bytes 1572868
  265.1 5.1 %copy-start.3 = (bf16[32,128,256]{1,2,0:T(8,128)(2,1)S(1)}, bf16[32,128,256]{1,2,0:T(8,128)(2,1)}, u32[]{:S(2)}) copy-start(bf16[32,128,256]{1,2,0:T(8,128)(2,1)} %copy.67) | copy-start | bytes 6291460
  271.8 99.4 %reduce-scatter.2.cloned.1.call-start = ((), (), s32[]{:S(2)}) async-start(), calls=%async_computation.5 | async-start | bytes 2359296 | tf_op jit(solution)/shard_map/reduce_scatter | solution.py:134
Sparse Core Ops, SparseCore 0:
  271.9 50.7 all-gather.1
  328.7 42.4 reduce-scatter.1
